TPU v7x, 32 devices: a whole 2x2x4 slice. The times are simulated.
32 devices in a mesh: ctx: 8 (over y, x, core), tp: 4 (over z).
Axes of the slice: x: 2, y: 2, z: 4, core: 2. Of those that a mesh axis runs over, the one named last changes fastest.
Arguments:
- tokens: bfloat16 [4096, 2048], P(('ctx', 'tp')), may hold values from -8 to 8
- projection: bfloat16 [2048, 640], P(None, 'tp'), may hold values from -0.125 to 0.125
- conv_weight: float32 [4, 640], P(None, 'tp'), may hold values from -2.5 to 2.5
Outputs:
- attended: bfloat16 [4096, 512], P('ctx', 'tp')
All inputs are finite; a program needn't handle non-finite values.
Results may differ from a plain program's by a relative error of at most 0.0032.
The roundings to bfloat16 on the way count: a program that leaves them out, or rounds other values in their place, can miss the bound.
Values may be sent and summed in bfloat16 or wider, within the bound.
No kernel may reach another device: no remote copies, remote signals or barrier semaphores. Data moves between devices by JAX's collectives and lax.ppermute only.
A program may use at most 64 MiB of HBM per device.

v0:
```python
import math
import jax
import jax.numpy as jnp
from jax import lax
from jax.sharding import PartitionSpec as P

FEAT = 16


def passed_along(shard, axis, by):
    length = lax.axis_size(axis)
    pairs = [(i, i + by) for i in range(length) if 0 <= i + by < length]
    return lax.ppermute(shard, axis, pairs)


def taylor(raw_vals):
    num_rows, width_feat = raw_vals.shape
    linear = raw_vals * width_feat ** (-0.25)
    quadratic = (raw_vals[:, :, None] * raw_vals[:, None, :]).reshape(
        num_rows, width_feat * width_feat
    )
    quadratic = quadratic * (1.0 / (math.sqrt(2.0) * math.sqrt(width_feat)))
    ones_col = jnp.ones((num_rows, 1), jnp.float32)
    return jnp.concatenate([ones_col, linear, quadratic], axis=1).astype(jnp.bfloat16)


def per_device(tokens, projection, conv_weight):
    kernel_len = conv_weight.shape[0]
    conv_lag = kernel_len - 1
    row_width = projection.shape[1]
    highest = lax.Precision.HIGHEST
    projected = jnp.dot(
        lax.all_gather(tokens, "tp", axis=0, tiled=True),
        projection,
        preferred_element_type=jnp.float32,
    ).astype(jnp.bfloat16)
    rim_rows = passed_along(projected[projected.shape[0] - conv_lag :], "ctx", 1)
    local_rows = projected.shape[0]
    padded = jnp.concatenate([rim_rows, projected], axis=0).astype(jnp.float32)
    convolved = jnp.zeros((local_rows, row_width), jnp.float32)
    for offset in range(kernel_len):
        convolved = (
            convolved
            + conv_weight[offset] * padded[conv_lag - offset : conv_lag - offset + local_rows]
        )
    feat_query = taylor(convolved[:, :FEAT])
    feat_key = taylor(convolved[:, FEAT : 2 * FEAT])
    values = convolved[:, 2 * FEAT :].astype(jnp.bfloat16)
    num_feat = feat_key.shape[1]
    val_width = values.shape[1]
    local_state = jnp.einsum("tp,tv->pv", feat_key, values, preferred_element_type=jnp.float32)
    local_total = jnp.sum(feat_key.astype(jnp.float32), axis=0)
    empty_state = jnp.zeros((num_feat, val_width), jnp.float32)
    empty_total = jnp.zeros((num_feat,), jnp.float32)
    position = lax.axis_index("ctx")
    states = lax.all_gather(local_state[None], "ctx", axis=0, tiled=True)
    sums = lax.all_gather(local_total[None], "ctx", axis=0, tiled=True)
    earlier_mask = jnp.arange(states.shape[0]) < position
    new_state = jnp.sum(jnp.where(earlier_mask[:, None, None], states, 0.0), axis=0)
    new_total = jnp.sum(jnp.where(earlier_mask[:, None], sums, 0.0), axis=0)
    block_rows = min(local_rows, 768)
    num_blocks = local_rows // block_rows
    query_blocks = feat_query.reshape(num_blocks, block_rows, num_feat)
    key_blocks = feat_key.reshape(num_blocks, block_rows, num_feat)
    value_blocks = values.reshape(num_blocks, block_rows, val_width)
    causal = jnp.arange(block_rows)[:, None] >= jnp.arange(block_rows)[None, :]

    def block_step(carried, blocks):
        run_state, run_total = carried
        query_blk, key_blk, value_blk = blocks
        scores = jnp.einsum("ip,jp->ij", query_blk, key_blk, preferred_element_type=jnp.float32)
        scores = jnp.where(causal, scores, 0.0)
        numerator = jnp.dot(
            scores.astype(jnp.bfloat16), value_blk, preferred_element_type=jnp.float32
        )
        denominator = jnp.sum(scores, axis=1)
        query_wide = query_blk.astype(jnp.float32)
        numerator = numerator + jnp.dot(query_wide, run_state, precision=highest)
        denominator = denominator + jnp.dot(query_wide, run_total, precision=highest)
        run_state = run_state + jnp.einsum(
            "tp,tv->pv", key_blk, value_blk, preferred_element_type=jnp.float32
        )
        run_total = run_total + jnp.sum(key_blk.astype(jnp.float32), axis=0)
        return ((run_state, run_total), (numerator, denominator))

    _, (numerator, denominator) = lax.scan(
        block_step, (empty_state, empty_total), (query_blocks, key_blocks, value_blocks)
    )
    numerator = numerator.reshape(local_rows, val_width)
    denominator = denominator.reshape(local_rows)
    query_wide = feat_query.astype(jnp.float32)
    numerator = numerator + jnp.dot(query_wide, new_state, precision=highest)
    denominator = denominator + jnp.dot(query_wide, new_total, precision=highest)
    return (numerator / denominator[:, None]).astype(jnp.bfloat16)


def solution(mesh):
    return jax.shard_map(
        per_device,
        mesh=mesh,
        in_specs=(P(("ctx", "tp"), None), P(None, "tp"), P(None, "tp")),
        out_specs=P("ctx", "tp"),
        check_vma=False,
    )
```

profile of v0, /device:TPU:0, one launch (start us, length us, event | category | flops | bytes accessed | tf_op | source)
XLA Modules:
  0.0 101.6 jit_solution(15885712231923730799)
XLA Ops:
  6.5 0.0 copy-start
  6.5 0.0 all-gather.6.cloned.1.call-start
  6.5 0.7 all-gather.6.cloned.1.call-update
  7.3 0.0 all-gather.8.cloned.1.call-start
  7.3 0.8 fusion.12
  8.2 0.0 copy-start.1
  8.2 49.2 %all-gather.6.cloned.1.call-done = bf16[512,2048]{1,0:T(8,128)(2,1)} async-done(((bf16[128,2048]{1,0:T(8,128)(2,1)}), bf16[512,2048]{1,0:T(8,128)(2,1)}) %all-gather.6.cloned.1.call-update) | async-done | bytes 2097168 | tf_op jit(solution)/shard_map/all_gather | solution.py:33
  57.3 0.0 copy-done
  57.3 2.4 %convolution_convert_fusion = bf16[512,160]{0,1:T(8,128)(2,1)S(1)} fusion(bf16[512,2048]{1,0:T(8,128)(2,1)} %all-gather.6.cloned.1.call-done, bf16[2048,160]{0,1:T(8,128)(2,1)S(1)} %copy-done), kind=kOutput, calls=%fused_computation.4 | convolution fusion | flops 335626240 | bytes 2916352 | tf_op jit(solution)/shard_map/dot_general | solution.py:32
  59.8 0.1 slice.49
  59.8 1.6 %collective-permute-start = (bf16[3,160]{0,1:T(8,128)(2,1)S(1)}, bf16[3,160]{0,1:T(8,128)(2,1)S(1)}, u32[]{:S(2)}, u32[]{:S(2)}) collective-permute-start(bf16[3,160]{0,1:T(8,128)(2,1)S(1)} %slice.49), channel_id=1, source_target_pairs={{0,4},{4,8},{8,12},{12,16},{16,20},{20,24},{24,28},{1,5},{5,9},{9,... | collective-permute-start | bytes 2888 | tf_op jit(solution)/shard_map/ppermute | solution.py:13
  61.4 0.0 copy-done.1
  61.5 0.6 dynamic-slice.3
  62.7 0.0 collective-permute-done
  62.7 0.1 maximum_convert_fusion
  62.8 0.4 fusion.4
  63.3 0.9 convolution_bitcast_fusion
  64.3 0.2 convert_reduce_fusion
  64.5 0.0 all-gather.8.cloned.1.call-update
  64.6 0.3 dynamic-update-slice
  64.8 24.9 %all-reduce = f32[2184]{0:T(1024)S(1)} all-reduce(f32[2184]{0:T(1024)S(1)} %dynamic-update-slice), channel_id=3, replica_groups=mesh['ctx'=8,'tp'=4] {'ctx'}, use_global_device_ids=true, to_apply=%add | all-reduce | flops 2184 | bytes 17472
  89.7 0.1 reshape.41
  89.8 0.1 select_reduce_fusion.1
  89.9 0.1 pad_maximum_fusion
  90.1 0.2 fusion.8
  90.3 0.2 fusion.14
  90.5 0.6 fusion.13
  91.1 0.3 fusion.2
  91.5 0.6 convolution_add_fusion.1
  92.1 0.0 all-gather.8.cloned.1.call-done
  92.1 1.4 %select_reduce_fusion = f32[273,128]{1,0:T(8,128)S(1)} fusion(f32[8,273,128]{2,1,0:T(8,128)} %all-gather.8.cloned.1.call-done, pred[8]{0:T(512)(128)(4,1)S(1)} %iota_compare_fusion.1), kind=kLoop, calls=%fused_computation.6 | loop fusion | flops 524160 | bytes 1257992 | tf_op jit(solution)/shard_map/reduce_sum | solution.py:59
  93.5 1.3 %fusion.1 = bf16[512,128]{1,0:T(8,128)(2,1)} fusion(f32[512,128]{1,0:T(8,128)S(1)} %convolution_add_fusion.1, bf16[512,273]{0,1:T(8,128)(2,1)S(1)} %pad_maximum_fusion, f32[273,128]{1,0:T(8,128)S(1)} %select_reduce_fusion, f32[512]{0:T(512)S(1)} %add_add_fusion), kind=kOutput, calls=%fused_computation.5 | convolution fusion | flops 214892544 | bytes 814592 | tf_op jit(solution)/shard_map/dot_general | solution.py:92
  (8 shorter events, 0.1 us)
Async XLA Ops:
  6.5 50.8 %copy-start = (bf16[2048,160]{0,1:T(8,128)(2,1)S(1)}, bf16[2048,160]{0,1:T(8,128)(2,1)}, u32[]{:S(2)}) copy-start(bf16[2048,160]{0,1:T(8,128)(2,1)} %param.4) | copy-start | bytes 1966084
  6.5 50.8 %all-gather.6.cloned.1.call-start = ((), (), s32[]{:S(2)}) async-start(), calls=%async_computation | async-start | bytes 2621440 | tf_op jit(solution)/shard_map/all_gather | solution.py:33
  7.3 84.8 %all-gather.8.cloned.1.call-start = ((), (), s32[]{:S(2)}) async-start(), calls=%async_computation.1 | async-start | bytes 1290240 | tf_op jit(solution)/shard_map/all_gather | solution.py:56
  8.2 53.3 %copy-start.1 = (u32[32]{0:T(128)S(1)}, u32[32]{0:T(128)}, u32[]{:S(2)}) copy-start(u32[32]{0:T(128)} %constant.37) | copy-start | bytes 388
  59.8 2.9 %collective-permute-start = (bf16[3,160]{0,1:T(8,128)(2,1)S(1)}, bf16[3,160]{0,1:T(8,128)(2,1)S(1)}, u32[]{:S(2)}, u32[]{:S(2)}) collective-permute-start(bf16[3,160]{0,1:T(8,128)(2,1)S(1)} %slice.49), channel_id=1, source_target_pairs={{0,4},{4,8},{8,12},{12,16},{16,20},{20,24},{24,28},{1,5},{5,9},{9,... | collective-permute-start | bytes 2888 | tf_op jit(solution)/shard_map/ppermute | solution.py:13
Sparse Core Ops, SparseCore 0:
  8.9 48.3 all-gather.5
  64.7 25.1 all-gather.7
where the time goes:
time: 102 us
  waiting for transfers between devices  49.9 us (49%)
  blocking collectives  24.9 us (24%)
  between operations  14.2 us (14%)
  matrix products  6.61 us (6%)
  other arithmetic  2.53 us (2%)
  local copies, waits for them, and re-layouts  1.89 us (2%)
  starting transfers between devices  1.61 us (2%)
    all_gather x1, waiting for transfers between devices, per_device(): lax.all_gather(tokens, 'tp', axis=0, tiled=True)  49.2 us
    unnamed x1, blocking collectives  24.9 us
    dot_general x1, matrix products, per_device(): jnp.dot(lax.all_gather(tokens, 'tp', axis=0, tiled=True), projection, pre...  2.43 us
  transfers between devices with their start and end apart: 3, of which 1 were waited for; matrix products, arithmetic and copies ran while one was open for 4% of the time, Pallas kernels for 0%

commit v1 on v0

--- a/solution.py
+++ b/solution.py
@@ -5,6 +5,23 @@
 from jax.sharding import PartitionSpec as P
 
 FEAT = 16
+
+
+def joined_along(blocks, dim):
+    blocks = jnp.moveaxis(blocks, 0, dim)
+    shape = blocks.shape
+    return blocks.reshape(*shape[:dim], shape[dim] * shape[dim + 1], *shape[dim + 2 :])
+
+
+def gather_around(value, axis, dim):
+    peers = lax.axis_size(axis)
+    upward = [(i, (i + 1) % peers) for i in range(peers)]
+    blocks = [value]
+    while len(blocks) < peers:
+        blocks.append(lax.ppermute(blocks[-1], axis, upward))
+    index = lax.axis_index(axis)
+    blocks = jnp.stack(blocks)[(index - jnp.arange(peers)) % peers]
+    return joined_along(blocks, dim)
 
 
 def passed_along(shard, axis, by):
@@ -30,9 +47,7 @@
     row_width = projection.shape[1]
     highest = lax.Precision.HIGHEST
     projected = jnp.dot(
-        lax.all_gather(tokens, "tp", axis=0, tiled=True),
-        projection,
-        preferred_element_type=jnp.float32,
+        gather_around(tokens, "tp", 0), projection, preferred_element_type=jnp.float32
     ).astype(jnp.bfloat16)
     rim_rows = passed_along(projected[projected.shape[0] - conv_lag :], "ctx", 1)
     local_rows = projected.shape[0]

time: 102 us -> 121 us (1.19)
  waiting for transfers between devices: 49.9 us -> 62.3 us
  local copies, waits for them, and re-layouts: 1.89 us -> 4.67 us
  starting transfers between devices: 1.61 us -> 4.35 us
  other arithmetic: 2.53 us -> 4.16 us
    all_gather x1 -> x0, waiting for transfers between devices: 49.2 us -> none  [per_device(): lax.all_gather(tokens, 'tp', axis=0, tiled=True)]
    ppermute x0 -> x3, waiting for transfers between devices: none -> 42.1 us  [gather_around(): blocks.append(lax.ppermute(blocks[-1], axis, upward))]
    all_gather x1, waiting for transfers between devices: 0.02 us -> 20.1 us  [per_device(): states = lax.all_gather(local_state[None], 'ctx', axis=0, tiled=True)]
    ppermute x0 -> x3, starting transfers between devices: none -> 3.06 us  [gather_around(): blocks.append(lax.ppermute(blocks[-1], axis, upward))]
    gather x0 -> x1, local copies, waits for them, and re-layouts: none -> 2.03 us  [gather_around(): blocks = jnp.stack(blocks)[(index - jnp.arange(peers)) % peers]]
    another operation x3 -> x4, other arithmetic: 0.11 us -> 1.73 us  [the longest x1 1.62 us: gather_around(): blocks = jnp.stack(blocks)[(index - jnp.arange(peers)) % peers]]
  transfers between devices with their start and end apart: 3 -> 5, of which waited for: 1 -> 4; matrix products, arithmetic and copies ran while one was open for 4% -> 3% of each run, Pallas kernels for 0% -> 0%
where the time goes in v1:
time: 121 us
  waiting for transfers between devices  62.3 us (51%)
  blocking collectives  24.4 us (20%)
  between operations  14.2 us (12%)
  matrix products  6.63 us (5%)
  local copies, waits for them, and re-layouts  4.67 us (4%)
  starting transfers between devices  4.35 us (4%)
  other arithmetic  4.16 us (3%)
    ppermute x3, waiting for transfers between devices, gather_around(): blocks.append(lax.ppermute(blocks[-1], axis, upward))  42.1 us
    unnamed x1, blocking collectives  24.4 us
    all_gather x1, waiting for transfers between devices, per_device(): states = lax.all_gather(local_state[None], 'ctx', axis=0, tiled=True)  20.1 us
    ppermute x3, starting transfers between devices, gather_around(): blocks.append(lax.ppermute(blocks[-1], axis, upward))  3.06 us
    dot_general x1, matrix products, per_device(): jnp.dot(gather_around(tokens, 'tp', 0), projection, preferred_element_typ...  2.45 us
  transfers between devices with their start and end apart: 5, of which 4 were waited for; matrix products, arithmetic and copies ran while one was open for 3% of the time, Pallas kernels for 0%

profile of v1, /device:TPU:0, one launch (start us, length us, event | category | flops | bytes accessed | tf_op | source)
XLA Modules:
  0.0 120.6 jit_solution(1843827754493620923)
XLA Ops:
  6.5 3.1 %collective-permute-start = (bf16[128,2048]{1,0:T(8,128)(2,1)}, bf16[128,2048]{1,0:T(8,128)(2,1)S(1)}, u32[]{:S(2)}, u32[]{:S(2)}) collective-permute-start(bf16[128,2048]{1,0:T(8,128)(2,1)} %param.3), channel_id=1, source_target_pairs={{0,1},{1,2},{2,3},{3,0},{4,5},{5,6},{6,7},{7,4},{8,9},{9,10},{10,1... | collective-permute-start | bytes 1572872 | tf_op jit(solution)/shard_map/ppermute | solution.py:21
  9.6 14.2 %collective-permute-done = bf16[128,2048]{1,0:T(8,128)(2,1)S(1)} collective-permute-done((bf16[128,2048]{1,0:T(8,128)(2,1)}, bf16[128,2048]{1,0:T(8,128)(2,1)S(1)}, u32[]{:S(2)}, u32[]{:S(2)}) %collective-permute-start) | collective-permute-done | bytes 524320 | tf_op jit(solution)/shard_map/ppermute | solution.py:21
  23.7 0.0 collective-permute-start.1
  23.8 14.9 %collective-permute-done.1 = bf16[128,2048]{1,0:T(8,128)(2,1)S(1)} collective-permute-done((bf16[128,2048]{1,0:T(8,128)(2,1)S(1)}, bf16[128,2048]{1,0:T(8,128)(2,1)S(1)}, u32[]{:S(2)}, u32[]{:S(2)}) %collective-permute-start.1) | collective-permute-done | bytes 524320 | tf_op jit(solution)/shard_map/ppermute | solution.py:21
  38.6 0.0 collective-permute-start.2
  38.7 0.9 fusion.14
  39.6 13.1 %collective-permute-done.2 = bf16[128,2048]{1,0:T(8,128)(2,1)S(1)} collective-permute-done((bf16[128,2048]{1,0:T(8,128)(2,1)S(1)}, bf16[128,2048]{1,0:T(8,128)(2,1)S(1)}, u32[]{:S(2)}, u32[]{:S(2)}) %collective-permute-start.2) | collective-permute-done | bytes 524320 | tf_op jit(solution)/shard_map/ppermute | solution.py:21
  52.7 0.8 copy-done.2
  53.5 1.6 %pad_maximum_fusion = bf16[4,128,2048]{2,1,0:T(8,128)(2,1)S(1)} fusion(bf16[1,128,2048]{2,1,0:T(8,128)(2,1)} %bitcast.37, bf16[1,128,2048]{2,1,0:T(8,128)(2,1)} %bitcast.36, bf16[1,128,2048]{2,1,0:T(8,128)(2,1)S(1)} %bitcast.35, bf16[1,128,2048]{2,1,0:T(8,128)(2,1)} %bitcast.34), kind=kLoop, calls=%fused_computation.1 | loop fusion | flops 3145728 | bytes 4194304 | tf_op jit(solution)/shard_map/stack | solution.py:23
  55.1 2.0 %gather_fusion = bf16[4,128,2048]{2,1,0:T(8,128)(2,1)} fusion(bf16[4,128,2048]{2,1,0:T(8,128)(2,1)S(1)} %pad_maximum_fusion, s32[1024]{0:T(1024)S(1)} %pad_clamp_fusion), kind=kCustom, calls=%fused_computation | custom fusion | bytes 4194320 | tf_op jit(solution)/shard_map/gather | solution.py:23
  57.1 2.4 %convolution_convert_fusion = bf16[512,160]{0,1:T(8,128)(2,1)S(1)} fusion(bf16[512,2048]{1,0:T(8,128)(2,1)} %bitcast.29, bf16[2048,160]{0,1:T(8,128)(2,1)S(1)} %copy-done), kind=kOutput, calls=%fused_computation.6 | convolution fusion | flops 335626240 | bytes 2916352 | tf_op jit(solution)/shard_map/dot_general | solution.py:49
  59.6 0.1 slice.51
  59.6 1.3 %collective-permute-start.3 = (bf16[3,160]{0,1:T(8,128)(2,1)S(1)}, bf16[3,160]{0,1:T(8,128)(2,1)S(1)}, u32[]{:S(2)}, u32[]{:S(2)}) collective-permute-start(bf16[3,160]{0,1:T(8,128)(2,1)S(1)} %slice.51), channel_id=1, source_target_pairs={{0,4},{4,8},{8,12},{12,16},{16,20},{20,24},{24,28},{1,5},{5,9},{9,... | collective-permute-start | bytes 2888 | tf_op jit(solution)/shard_map/ppermute | solution.py:30
  61.0 0.6 dynamic-slice.3
  62.2 0.1 maximum_convert_fusion
  62.4 0.4 fusion.4
  62.9 0.2 convert_reduce_fusion
  63.1 1.0 convolution_bitcast_fusion
  64.1 0.2 dynamic-update-slice
  64.2 24.4 %all-reduce = f32[2184]{0:T(1024)S(1)} all-reduce(f32[2184]{0:T(1024)S(1)} %dynamic-update-slice), channel_id=3, replica_groups=mesh['ctx'=8,'tp'=4] {'ctx'}, use_global_device_ids=true, to_apply=%add | all-reduce | flops 2184 | bytes 17472
  88.6 0.1 reshape.102
  88.7 0.0 all-gather.5.cloned.1.call-update
  88.8 0.1 select_reduce_fusion.1
  88.9 0.1 pad_maximum_fusion.1
  89.0 0.2 fusion.8
  89.3 0.2 fusion.16
  89.5 0.6 fusion.15
  90.1 0.3 fusion.2
  90.4 0.6 convolution_add_fusion.1
  91.0 20.1 %all-gather.5.cloned.1.call-done = f32[8,273,128]{2,1,0:T(8,128)} async-done(((f32[1,273,128]{2,1,0:T(8,128)}), f32[8,273,128]{2,1,0:T(8,128)}) %all-gather.5.cloned.1.call-update) | async-done | bytes 1118224 | tf_op jit(solution)/shard_map/all_gather | solution.py:71
  111.1 1.4 %select_reduce_fusion = f32[273,128]{1,0:T(8,128)S(1)} fusion(f32[8,273,128]{2,1,0:T(8,128)} %all-gather.5.cloned.1.call-done, pred[8]{0:T(512)(128)(4,1)S(1)} %iota_compare_fusion.1), kind=kLoop, calls=%fused_computation.8 | loop fusion | flops 524160 | bytes 1257992 | tf_op jit(solution)/shard_map/reduce_sum | solution.py:74
  112.5 1.3 %fusion.1 = bf16[512,128]{1,0:T(8,128)(2,1)} fusion(f32[512,128]{1,0:T(8,128)S(1)} %convolution_add_fusion.1, bf16[512,273]{0,1:T(8,128)(2,1)S(1)} %pad_maximum_fusion.1, f32[273,128]{1,0:T(8,128)S(1)} %select_reduce_fusion, f32[512]{0:T(512)S(1)} %add_add_fusion), kind=kOutput, calls=%fused_computation.7 | convolution fusion | flops 214892544 | bytes 814592 | tf_op jit(solution)/shard_map/dot_general | solution.py:107
  (19 shorter events, 0.2 us)
Async XLA Ops:
  6.5 50.6 %copy-start = (bf16[2048,160]{0,1:T(8,128)(2,1)S(1)}, bf16[2048,160]{0,1:T(8,128)(2,1)}, u32[]{:S(2)}) copy-start(bf16[2048,160]{0,1:T(8,128)(2,1)} %param.4) | copy-start | bytes 1966084
  6.5 104.6 %all-gather.5.cloned.1.call-start = ((), (), s32[]{:S(2)}) async-start(), calls=%async_computation | async-start | bytes 1290240 | tf_op jit(solution)/shard_map/all_gather | solution.py:71
  6.5 17.2 %collective-permute-start = (bf16[128,2048]{1,0:T(8,128)(2,1)}, bf16[128,2048]{1,0:T(8,128)(2,1)S(1)}, u32[]{:S(2)}, u32[]{:S(2)}) collective-permute-start(bf16[128,2048]{1,0:T(8,128)(2,1)} %param.3), channel_id=1, source_target_pairs={{0,1},{1,2},{2,3},{3,0},{4,5},{5,6},{6,7},{7,4},{8,9},{9,10},{10,1... | collective-permute-start | bytes 1572872 | tf_op jit(solution)/shard_map/ppermute | solution.py:21
  23.7 14.9 %collective-permute-start.1 = (bf16[128,2048]{1,0:T(8,128)(2,1)S(1)}, bf16[128,2048]{1,0:T(8,128)(2,1)S(1)}, u32[]{:S(2)}, u32[]{:S(2)}) collective-permute-start(bf16[128,2048]{1,0:T(8,128)(2,1)S(1)} %collective-permute-done), channel_id=1, source_target_pairs={{0,1},{1,2},{2,3},{3,0},{4,5},{5,6},{6,7},{7,4},{8,9},{9,10},{10,1... | collective-permute-start | bytes 1572872 | tf_op jit(solution)/shard_map/ppermute | solution.py:21
  38.6 14.0 %copy-start.1 = (bf16[128,2048]{1,0:T(8,128)(2,1)}, bf16[128,2048]{1,0:T(8,128)(2,1)S(1)}, u32[]{:S(2)}) copy-start(bf16[128,2048]{1,0:T(8,128)(2,1)S(1)} %collective-permute-done.1) | copy-start | bytes 1572868
  38.6 14.0 %collective-permute-start.2 = (bf16[128,2048]{1,0:T(8,128)(2,1)S(1)}, bf16[128,2048]{1,0:T(8,128)(2,1)S(1)}, u32[]{:S(2)}, u32[]{:S(2)}) collective-permute-start(bf16[128,2048]{1,0:T(8,128)(2,1)S(1)} %collective-permute-done.1), channel_id=1, source_target_pairs={{0,1},{1,2},{2,3},{3,0},{4,5},{5,6},{6,7},{7,4},{8,9},{9,10},{10,1... | collective-permute-start | bytes 1572872 | tf_op jit(solution)/shard_map/ppermute | solution.py:21
  52.7 0.8 copy-start.2
  57.1 3.9 %copy-start.3 = (u32[32]{0:T(128)S(1)}, u32[32]{0:T(128)}, u32[]{:S(2)}) copy-start(u32[32]{0:T(128)} %constant.57) | copy-start | bytes 388
  59.6 2.6 %collective-permute-start.3 = (bf16[3,160]{0,1:T(8,128)(2,1)S(1)}, bf16[3,160]{0,1:T(8,128)(2,1)S(1)}, u32[]{:S(2)}, u32[]{:S(2)}) collective-permute-start(bf16[3,160]{0,1:T(8,128)(2,1)S(1)} %slice.51), channel_id=1, source_target_pairs={{0,4},{4,8},{8,12},{12,16},{16,20},{20,24},{24,28},{1,5},{5,9},{9,... | collective-permute-start | bytes 2888 | tf_op jit(solution)/shard_map/ppermute | solution.py:30
Sparse Core Ops, SparseCore 0:
  88.9 22.1 all-gather.4
